TPU v7x, 32 devices: a whole 2x2x4 slice. The times are simulated.
32 devices in a mesh: member: 4 (over y, x), space: 8 (over z, core).
Axes of the slice: x: 2, y: 2, z: 4, core: 2. Of those that a mesh axis runs over, the one named last changes fastest.
Arguments:
- features: bfloat16 [8, 32, 64, 1024], P('member', None, 'space'), may hold values from -6 to 6
- skip: bfloat16 [8, 32, 64, 1024], P('member', None, 'space'), may hold values from -6 to 6
- conv_weight: bfloat16 [3, 3, 32, 32], replicated, may hold values from -0.625 to 0.625
- out_weight: bfloat16 [2, 32], replicated, may hold values from -2 to 2
- target: float32 [2, 64, 1024], P(None, 'space'), may hold values from -12 to 12
Outputs:
- grad_input: bfloat16 [8, 32, 64, 1024], P('member', None, 'space')
All inputs are finite; a program needn't handle non-finite values.
Results may differ from a plain program's by a relative error of at most 0.012.
Values may be sent and summed in bfloat16 or wider, within the bound.
A program may use at most 64 MiB of HBM per device.

v0:
```python
import functools
import math

import jax
import jax.numpy as jnp
from jax import lax
from jax.experimental import pallas as pl
from jax.experimental.pallas import tpu as pltpu
from jax.sharding import PartitionSpec as P

root_coef = math.sqrt(2.0 / math.pi)
cubic_coef = 0.044715
smooth = 0.25
lane = 128
MESH = pl.DeviceIdType.MESH
F32 = jnp.float32
BF16 = jnp.bfloat16


def gelu_half(source, square):
    return 0.5 + 0.5 * jnp.tanh(source * (root_coef + (root_coef * cubic_coef) * square))


def gelu_value(source):
    return source * gelu_half(source, source * source)


def gelu_slope(source):
    square = source * source
    half = gelu_half(source, square)
    rate = 2.0 * root_coef + (6.0 * root_coef * cubic_coef) * square
    return half + (source * half) * ((1.0 - half) * rate)


def smooth_slope(source):
    return source * lax.rsqrt(source * source + smooth * smooth)


def dot(left, right):
    return lax.dot_general(left, right, (((1,), (0,)), ((), ())), preferred_element_type=F32)


def dot_nt(left, right):
    return lax.dot_general(left, right, (((1,), (1,)), ((), ())), preferred_element_type=F32)


def split_index(shape, dim, size):
    index = lax.broadcasted_iota(jnp.int32, shape, dim)
    if size & (size - 1) == 0:
        return lax.shift_right_logical(index, size.bit_length() - 1), index & (size - 1)
    return lax.div(index, size), lax.rem(index, size)


def shifted(value, step):
    count = value.shape[1]
    edge = jnp.zeros((value.shape[0], 1), value.dtype)
    if step == 1:
        return jnp.concatenate([value[:, 1:], edge], axis=1)
    return jnp.concatenate([edge, value[:, : count - 1]], axis=1)


def kernel(
    dims, x_hbm, skip_hbm, weight, out_w, target_hbm, out,
    x, skip, target, stk, hstk, pre, act, hs, hx, hse, hg, hgo, outs, osend, ybuf, gout, se, woe,
    wf, wfh, wb, wbh, wo, wot, sel,
    in_sem, hs_sem, hx_sem, gs_sem, hg_sem, as_sem, ar_sem, cs_sem, cr_sem,
):
    members, chans, rows, cols, peers, count, outn, chunk = dims
    full = chans * rows
    me = lax.axis_index("member")
    at = lax.axis_index("space")
    has_up = at > 0
    has_dn = at < count - 1
    up = {"space": lax.max(at - 1, 0)}
    dn = {"space": lax.min(at + 1, count - 1)}

    loads = [pltpu.make_async_copy(x_hbm.at[m], x.at[m], in_sem.at[m]) for m in range(members)]
    skips = [
        pltpu.make_async_copy(skip_hbm.at[m], skip.at[m], in_sem.at[members + m])
        for m in range(members)
    ]
    tgt = pltpu.make_async_copy(target_hbm, target, in_sem.at[2 * members])
    for c in loads + skips + [tgt]:
        c.start()

    barrier = pltpu.get_barrier_semaphore()
    for d in range(1, peers):
        pl.semaphore_signal(
            barrier, inc=1, device_id={"member": lax.rem(me + d, peers)}, device_id_type=MESH
        )

    @pl.when(has_up)
    def _():
        pl.semaphore_signal(barrier, inc=1, device_id=up, device_id_type=MESH)

    @pl.when(has_dn)
    def _():
        pl.semaphore_signal(barrier, inc=1, device_id=dn, device_id_type=MESH)

    chan, row = split_index((2 * chans, full), 1, rows)
    half, pick = split_index((2 * chans, full), 0, chans)
    sel[...] = (
        (chan == pick) & (row == jnp.where(half == 0, 0, rows - 1))
    ).astype(F32).astype(BF16)

    left_chan, left_row = split_index((full, chans), 0, rows)
    spread = (left_chan == lax.broadcasted_iota(jnp.int32, (full, chans), 1)).astype(F32)
    spread = spread.astype(BF16)
    _, row_a = split_index((full, full), 0, rows)
    _, row_b = split_index((full, full), 1, rows)
    gap = row_b - row_a

    def place(slot):
        shape = (chans, 6 * chans)
        return (
            lax.broadcasted_iota(jnp.int32, shape, 1)
            == lax.broadcasted_iota(jnp.int32, shape, 0) + slot * chans
        ).astype(F32).astype(BF16)

    def build(main, halo, flipped):
        edges = jnp.zeros((full, 6 * chans), F32)
        for dc in range(3):
            band = jnp.zeros((full, full), F32)
            for dr in range(3):
                offset = 1 - dr if flipped else dr - 1
                if flipped and offset == 0:
                    continue
                part = (dot_nt if flipped else dot)(spread, weight[dr, dc]).astype(BF16)
                if not flipped:
                    band = jnp.where(gap == offset, dot_nt(part, spread), band)
                if offset != 0:
                    kept = jnp.where(
                        left_row == (0 if offset < 0 else rows - 1), part.astype(F32), 0.0
                    ).astype(BF16)
                    edges = edges + dot(kept, place(2 * dc + (0 if offset < 0 else 1)))
            span = slice(dc * full, (dc + 1) * full)
            main[:, span] = wf[:, span].T if flipped else band.astype(BF16)
        halo[...] = edges.astype(BF16)

    pl.semaphore_wait(
        barrier, peers - 1 + has_up.astype(jnp.int32) + has_dn.astype(jnp.int32)
    )

    def edge_of(src, m, half):
        return src.at[m, half] if len(src.shape) == 4 else src.at[m]

    def halo_copies(m, src, dst, send, recv):
        to_up = pltpu.make_async_remote_copy(
            src_ref=edge_of(src, m, 0), dst_ref=dst.at[m, 1], send_sem=send.at[m, 0],
            recv_sem=recv.at[m, 1], device_id=up, device_id_type=MESH,
        )
        to_dn = pltpu.make_async_remote_copy(
            src_ref=edge_of(src, m, 1), dst_ref=dst.at[m, 0], send_sem=send.at[m, 1],
            recv_sem=recv.at[m, 0], device_id=dn, device_id_type=MESH,
        )
        return to_up, to_dn

    def halo_start(m, src, dst, send, recv):
        to_up, to_dn = halo_copies(m, src, dst, send, recv)

        @pl.when(has_up)
        def _():
            to_up.start()

        @pl.when(has_dn)
        def _():
            to_dn.start()

        @pl.when(jnp.logical_not(has_up))
        def _():
            dst[m, 0] = jnp.zeros(dst.shape[2:], dst.dtype)

        @pl.when(jnp.logical_not(has_dn))
        def _():
            dst[m, 1] = jnp.zeros(dst.shape[2:], dst.dtype)

    def halo_wait(m, src, dst, send, recv, which):
        to_up, to_dn = halo_copies(m, src, dst, send, recv)

        @pl.when(has_up)
        def _():
            to_up.wait_send() if which == "send" else to_dn.wait_recv()

        @pl.when(has_dn)
        def _():
            to_dn.wait_send() if which == "send" else to_up.wait_recv()

    def send_edges(m, source, store, dst, send, recv):
        edge = dot(sel[...], source).astype(BF16)
        store[m, 0] = edge[:chans]
        store[m, 1] = edge[chans:]
        halo_start(m, store, dst, send, recv)

    def stack_halo(m, halo, order):
        both = jnp.concatenate([halo[m, 0], halo[m, 1]], axis=0)
        for slot, step in enumerate(order):
            value = both if step == 0 else shifted(both, step)
            hstk[m, slot * 2 * chans : (slot + 1) * 2 * chans, :] = value

    def stack_main(m, value, order):
        for slot, step in enumerate(order):
            stk[m, slot * full : (slot + 1) * full, :] = value if step == 0 else shifted(value, step)

    spans = [slice(n, n + chunk) for n in range(0, cols, chunk)]

    def get(m, span, lines=slice(None)):
        tiles = range(span.start // lane, span.stop // lane)
        return jnp.concatenate([pre[m, tile, lines, :] for tile in tiles], axis=1)

    def put(m, span, value, lines=slice(None)):
        for k, tile in enumerate(range(span.start // lane, span.stop // lane)):
            pre[m, tile, lines, :] = value[:, k * lane : (k + 1) * lane]

    for m in range(members):
        loads[m].wait()
        send_edges(m, x[m], hs, hx, hs_sem, hx_sem)
    build(wf, wfh, False)

    out_k, _ = split_index((outn * rows, chans), 0, rows)
    lines = jnp.zeros((outn * rows, chans), F32)
    for k in range(outn):
        lines = jnp.where(out_k == k, out_w[k : k + 1, :].astype(F32), lines)
    lines = lines.astype(BF16)
    _, oa = split_index((outn * rows, full), 0, rows)
    _, ob = split_index((outn * rows, full), 1, rows)
    wo[...] = jnp.where(oa == ob, dot_nt(lines, spread), 0.0).astype(BF16)
    _, ta = split_index((full, outn * rows), 0, rows)
    _, tb = split_index((full, outn * rows), 1, rows)
    wot[...] = jnp.where(ta == tb, dot_nt(spread, lines), 0.0).astype(BF16)
    for m in range(members):
        stack_main(m, x[m], (-1, 0, 1))
        skips[m].wait()
        for span in spans:
            put(m, span, dot(wf[...], stk[m, :, span]) + skip[m, :, span].astype(F32))

    parts = [slice(n, n + cols // 2) for n in range(0, cols, cols // 2)]

    def gather_copy(m, part, d):
        return pltpu.make_async_remote_copy(
            src_ref=osend.at[m, :, parts[part]],
            dst_ref=ybuf.at[d, m, :, parts[part]],
            send_sem=as_sem.at[m, part, d], recv_sem=ar_sem.at[m, part, d],
            device_id={"member": lax.rem(me + d, peers)}, device_id_type=MESH,
        )

    for m in range(members):
        halo_wait(m, hs, hx, hs_sem, hx_sem, "recv")
        stack_halo(m, hx, (-1, 0, 1))
        for part, range_of in enumerate(parts):
            for n in range(range_of.start, range_of.stop, chunk):
                span = slice(n, n + chunk)
                total = get(m, span) + dot(wfh[...], hstk[m, :, span])
                put(m, span, total)
                value = dot(wo[...], gelu_value(total).astype(BF16))
                outs[m, :, span] = value
                osend[m, :, span] = value.astype(BF16)
            for d in range(1, peers):
                gather_copy(m, part, d).start()
    block = 8 * rows
    for m in range(members):
        for n in range(0, full, block):
            for span in spans:
                lines = slice(n, n + block)
                put(m, span, gelu_slope(get(m, span, lines)), lines)
        for half in range(2):
            for tile in range(cols // lane):
                kept = pre[m, tile, pl.ds(half * (rows - 1), chans, stride=rows), :]
                se[m, half, :, tile * lane : (tile + 1) * lane] = kept
        halo_start(m, se, hse, gs_sem, hg_sem)
    build(wb, wbh, True)
    woe[...] = dot(sel[...], wot[...]).astype(BF16)

    tgt.wait()
    total_members = peers * members
    for part in range(2):
        for d in range(1, peers):
            for m in range(members):
                gather_copy(m, part, d).wait_recv()
        for n in range(parts[part].start, parts[part].stop, chunk):
            span = slice(n, n + chunk)
            own = [outs[m, :, span] for m in range(members)]
            pairs = [smooth_slope(v - v) for v in own]
            for i in range(members):
                for j in range(i):
                    term = smooth_slope(own[i] - own[j])
                    pairs[i] = pairs[i] + term
                    pairs[j] = pairs[j] - term
            for d in range(1, peers):
                for j in range(members):
                    other = ybuf[d, j, :, span].astype(F32)
                    for i in range(members):
                        pairs[i] = pairs[i] + smooth_slope(own[i] - other)
            for i in range(members):
                gout[i, :, span] = (
                    smooth_slope(own[i] - target[:, span]) - pairs[i] / (total_members - 1)
                ).astype(BF16)

    for m in range(members):
        halo_start(m, gout, hgo, cs_sem, cr_sem)
    for m in range(members):
        for span in spans:
            grad = dot(wot[...], gout[m, :, span])
            act[m, :, span] = (grad * get(m, span)).astype(BF16)
    for m in range(members):
        stack_main(m, act[m], (1, 0, -1))
        for span in spans:
            put(m, span, dot(wb[...], stk[m, :, span]))
    for m in range(members):
        halo_wait(m, se, hse, gs_sem, hg_sem, "recv")
        halo_wait(m, gout, hgo, cs_sem, cr_sem, "recv")
        for half in range(2):
            far = woe[(1 - half) * chans : (2 - half) * chans, :]
            hg[m, half] = (dot(far, hgo[m, half]) * hse[m, half]).astype(BF16)
        stack_halo(m, hg, (1, 0, -1))
        for span in spans:
            out[m, :, span] = (get(m, span) + dot(wbh[...], hstk[m, :, span])).astype(BF16)

    for m in range(members):
        halo_wait(m, hs, hx, hs_sem, hx_sem, "send")
        halo_wait(m, se, hse, gs_sem, hg_sem, "send")
        halo_wait(m, gout, hgo, cs_sem, cr_sem, "send")
        for part in range(2):
            for d in range(1, peers):
                gather_copy(m, part, d).wait_send()


def local(features, skip, conv_weight, out_weight, target):
    members, chans, rows, cols = features.shape
    outn = out_weight.shape[0]
    peers = lax.axis_size("member")
    count = lax.axis_size("space")
    full = chans * rows
    chunk = min(cols, 256)
    dims = (members, chans, rows, cols, peers, count, outn, chunk)
    dma = pltpu.SemaphoreType.DMA
    anywhere = pl.BlockSpec(memory_space=pltpu.HBM)
    vmem = pl.BlockSpec(memory_space=pltpu.VMEM)
    result = pl.pallas_call(
        functools.partial(kernel, dims),
        out_shape=pltpu.VMEM((members, full, cols), BF16),
        in_specs=[anywhere, anywhere, vmem, vmem, anywhere],
        out_specs=vmem,
        scratch_shapes=[
            pltpu.VMEM((members, full, cols), BF16),
            pltpu.VMEM((members, full, cols), BF16),
            pltpu.VMEM((outn * rows, cols), F32),
            pltpu.VMEM((members, 3 * full, cols), BF16),
            pltpu.VMEM((members, 6 * chans, cols), BF16),
            pltpu.VMEM((members, cols // lane, full, lane), F32),
            pltpu.VMEM((members, full, cols), BF16),
            pltpu.VMEM((members, 2, chans, cols), BF16),
            pltpu.VMEM((members, 2, chans, cols), BF16),
            pltpu.VMEM((members, 2, chans, cols), F32),
            pltpu.VMEM((members, 2, chans, cols), BF16),
            pltpu.VMEM((members, 2, outn * rows, cols), BF16),
            pltpu.VMEM((members, outn * rows, cols), F32),
            pltpu.VMEM((members, outn * rows, cols), BF16),
            pltpu.VMEM((peers, members, outn * rows, cols), BF16),
            pltpu.VMEM((members, outn * rows, cols), BF16),
            pltpu.VMEM((members, 2, chans, cols), F32),
            pltpu.VMEM((2 * chans, outn * rows), BF16),
            pltpu.VMEM((full, 3 * full), BF16),
            pltpu.VMEM((full, 6 * chans), BF16),
            pltpu.VMEM((full, 3 * full), BF16),
            pltpu.VMEM((full, 6 * chans), BF16),
            pltpu.VMEM((outn * rows, full), BF16),
            pltpu.VMEM((full, outn * rows), BF16),
            pltpu.VMEM((2 * chans, full), BF16),
            dma((2 * members + 1,)),
            dma((members, 2)),
            dma((members, 2)),
            dma((members, 2)),
            dma((members, 2)),
            dma((members, 2, peers)),
            dma((members, 2, peers)),
            dma((members, 2)),
            dma((members, 2)),
        ],
        compiler_params=pltpu.CompilerParams(collective_id=0, has_side_effects=True, vmem_limit_bytes=58 * 2**20),
    )(
        features.reshape(members, full, cols),
        skip.reshape(members, full, cols),
        conv_weight,
        out_weight,
        target.reshape(outn * rows, cols),
    )
    return result.reshape(members, chans, rows, cols)


def solution(mesh):
    placed = (
        P("member", None, "space", None),
        P("member", None, "space", None),
        P(),
        P(),
        P(None, "space", None),
    )
    return jax.shard_map(
        local,
        mesh=mesh,
        in_specs=placed,
        out_specs=P("member", None, "space", None),
        check_vma=False,
    )
```

profile of v0, /device:TPU:1, one launch (start us, length us, event | category | flops | bytes accessed | tf_op | source)
XLA Modules:
  0.0 19.1 jit_solution(6089267325969973791)
XLA Ops:
  0.0 18.1 %shard_map.55 = bf16[2,256,1024]{2,1,0:T(8,128)(2,1)S(1)} custom-call(bf16[2,256,1024]{2,1,0:T(8,128)(2,1)} %bitcast.5, bf16[2,256,1024]{2,1,0:T(8,128)(2,1)} %bitcast.6, bf16[3,3,32,32]{3,2,1,0:T(8,128)(2,1)} %weight.1, bf16[2,32]{1,0:T(2,128)(2,1)} %out_w.1, f32[16,1024]{1,0:T(8,128)} %bitcast.7), custom_call_target="tpu_custom_call" | custom-call | tf_op jit(solution)/shard_map/pallas_call | solution.py:338
  18.1 1.0 %copy.7 = bf16[2,32,8,1024]{3,2,1,0:T(8,128)(2,1)} copy(bf16[2,32,8,1024]{3,2,1,0:T(8,128)(2,1)S(1)} %bitcast.4) | data formatting | bytes 2097152
where the time goes:
time: 19.2 us; the launch traced here: 19.1 us
  Pallas kernels  18.1 us (94%)
  local copies, waits for them, and re-layouts  0.97 us (5%)
    pallas_call x1, Pallas kernels, local(): pl.pallas_call(functools.partial(kernel, dims), out_shape=pltpu.VMEM((mem...  18.1 us
    unnamed x1, local copies, waits for them, and re-layouts  0.97 us

commit v1 on v0

v1 whole, which is shorter than its diff:
```python
import functools
import math

import jax
import jax.numpy as jnp
from jax import lax
from jax.experimental import pallas as pl
from jax.experimental.pallas import tpu as pltpu
from jax.sharding import PartitionSpec as P

root_coef = math.sqrt(2.0 / math.pi)
cubic_coef = 0.044715
smooth = 0.25
lane = 128
MESH = pl.DeviceIdType.MESH
F32 = jnp.float32
BF16 = jnp.bfloat16


def gelu_half(source, square):
    return 0.5 + 0.5 * jnp.tanh(source * (root_coef + (root_coef * cubic_coef) * square))


def gelu_value(source):
    return source * gelu_half(source, source * source)


def gelu_slope(source):
    square = source * source
    half = gelu_half(source, square)
    rate = 2.0 * root_coef + (6.0 * root_coef * cubic_coef) * square
    return half + (source * half) * ((1.0 - half) * rate)


def smooth_slope(source):
    return source * lax.rsqrt(source * source + smooth * smooth)


def dot(left, right):
    return lax.dot_general(left, right, (((1,), (0,)), ((), ())), preferred_element_type=F32)


def dot_nt(left, right):
    return lax.dot_general(left, right, (((1,), (1,)), ((), ())), preferred_element_type=F32)


def split_index(shape, dim, size):
    index = lax.broadcasted_iota(jnp.int32, shape, dim)
    if size & (size - 1) == 0:
        return lax.shift_right_logical(index, size.bit_length() - 1), index & (size - 1)
    return lax.div(index, size), lax.rem(index, size)


def shifted(value, step):
    count = value.shape[1]
    edge = jnp.zeros((value.shape[0], 1), value.dtype)
    if step == 1:
        return jnp.concatenate([value[:, 1:], edge], axis=1)
    return jnp.concatenate([edge, value[:, : count - 1]], axis=1)


def kernel(
    dims, x_hbm, skip_hbm, weight_hbm, out_w_hbm, target_hbm, pre, hgk, wbh,
    x, skip, weight, out_w, target, hstk, act, slope, hs, hx, hse, hgo, outs, osend, ybuf,
    gout, gsend, se, wf, wfh, wb, band, wo, wcol, wrow, sel,
    in_sem, hs_sem, hx_sem, gs_sem, hg_sem, as_sem, ar_sem, cs_sem, cr_sem,
):
    members, chans, rows, cols, peers, count, outn, chunk = dims
    full = chans * rows
    me = lax.axis_index("member")
    at = lax.axis_index("space")
    has_up = at > 0
    has_dn = at < count - 1
    up = {"space": lax.max(at - 1, 0)}
    dn = {"space": lax.min(at + 1, count - 1)}

    loads = [pltpu.make_async_copy(x_hbm.at[m], x.at[m], in_sem.at[m]) for m in range(members)]
    skips = [
        pltpu.make_async_copy(skip_hbm.at[m], skip.at[m], in_sem.at[members + m])
        for m in range(members)
    ]
    tgt = pltpu.make_async_copy(target_hbm, target, in_sem.at[2 * members])
    taps = pltpu.make_async_copy(weight_hbm, weight, in_sem.at[2 * members + 1])
    heads = pltpu.make_async_copy(out_w_hbm, out_w, in_sem.at[2 * members + 2])
    for c in loads[:1] + [taps, heads] + loads[1:] + skips + [tgt]:
        c.start()

    barrier = pltpu.get_barrier_semaphore()
    for d in range(1, peers):
        pl.semaphore_signal(
            barrier, inc=1, device_id={"member": lax.rem(me + d, peers)}, device_id_type=MESH
        )

    @pl.when(has_up)
    def _():
        pl.semaphore_signal(barrier, inc=1, device_id=up, device_id_type=MESH)

    @pl.when(has_dn)
    def _():
        pl.semaphore_signal(barrier, inc=1, device_id=dn, device_id_type=MESH)

    chan, row = split_index((2 * chans, full), 1, rows)
    half, pick = split_index((2 * chans, full), 0, chans)
    sel[...] = (
        (chan == pick) & (row == jnp.where(half == 0, 0, rows - 1))
    ).astype(F32).astype(BF16)

    left_chan, left_row = split_index((full, chans), 0, rows)
    spread = (left_chan == lax.broadcasted_iota(jnp.int32, (full, chans), 1)).astype(F32)
    spread_first = jnp.where(left_row == 0, spread, 0.0).astype(BF16)
    spread_last = jnp.where(left_row == rows - 1, spread, 0.0).astype(BF16)
    spread = spread.astype(BF16)

    def build_forward():
        taps.wait()
        wide = dot_nt(weight[...].reshape(9 * chans, chans), spread)
        lane_row = lax.broadcasted_iota(jnp.int32, (chans, lane), 1) & (rows - 1)
        for dc in range(3):
            for tile in range(full // lane):
                cut = slice(tile * lane, (tile + 1) * lane)
                tap = [wide[(3 * dr + dc) * chans : (3 * dr + dc + 1) * chans, cut] for dr in range(3)]
                for r in range(rows):
                    line = jnp.where(lane_row == r, tap[1], 0.0)
                    if r > 0:
                        line = jnp.where(lane_row == r - 1, tap[0], line)
                    if r < rows - 1:
                        line = jnp.where(lane_row == r + 1, tap[2], line)
                    band[dc, tile, pl.ds(r, chans, stride=rows), :] = line
                wf[:, dc * full + tile * lane : dc * full + (tile + 1) * lane] = band[
                    dc, tile
                ].astype(BF16)

    def build_edges(halo, flipped):
        pieces = []
        for dc in range(3):
            for dr in (2, 0) if flipped else (0, 2):
                tap = weight[dr, dc].astype(F32)
                pieces.append(tap.T if flipped else tap)
        line = jnp.concatenate(pieces, axis=1)
        slot, _ = split_index((chans, 6 * chans), 1, chans)
        first = jnp.where(slot & 1 == 0, line, 0.0).astype(BF16)
        last = jnp.where(slot & 1 == 1, line, 0.0).astype(BF16)
        halo[...] = dot(spread_first, first).astype(BF16) + dot(spread_last, last).astype(BF16)

    def build_backward():
        for dc in range(3):
            span = slice(dc * full, (dc + 1) * full)
            wb[:, span] = wf[:, span].T

    for absent, side in ((jnp.logical_not(has_up), 0), (jnp.logical_not(has_dn), 1)):

        @pl.when(absent)
        def _(side=side):
            for landing in (hx, hse, hgo):
                for m in range(members):
                    landing[m, side] = jnp.zeros(landing.shape[2:], landing.dtype)

    pl.semaphore_wait(
        barrier, peers - 1 + has_up.astype(jnp.int32) + has_dn.astype(jnp.int32)
    )

    def edge_of(src, m, half):
        return src.at[m, half] if len(src.shape) == 4 else src.at[m]

    def halo_copies(m, src, dst, send, recv):
        to_up = pltpu.make_async_remote_copy(
            src_ref=edge_of(src, m, 0), dst_ref=dst.at[m, 1], send_sem=send.at[m, 0],
            recv_sem=recv.at[m, 1], device_id=up, device_id_type=MESH,
        )
        to_dn = pltpu.make_async_remote_copy(
            src_ref=edge_of(src, m, 1), dst_ref=dst.at[m, 0], send_sem=send.at[m, 1],
            recv_sem=recv.at[m, 0], device_id=dn, device_id_type=MESH,
        )
        return to_up, to_dn

    def halo_start(which, src, dst, send, recv):
        copies = [halo_copies(m, src, dst, send, recv) for m in which]

        @pl.when(has_up)
        def _():
            for to_up, _ in copies:
                to_up.start()

        @pl.when(has_dn)
        def _():
            for _, to_dn in copies:
                to_dn.start()

    def halo_wait(which, exchanges, kind):
        copies = [halo_copies(m, *exchange) for exchange in exchanges for m in which]

        @pl.when(has_up)
        def _():
            for to_up, to_dn in copies:
                to_up.wait_send() if kind == "send" else to_dn.wait_recv()

        @pl.when(has_dn)
        def _():
            for to_up, to_dn in copies:
                to_dn.wait_send() if kind == "send" else to_up.wait_recv()

    def send_edges(m, source, store, dst, send, recv):
        edge = dot(sel[...], source).astype(BF16)
        store[m, 0] = edge[:chans]
        store[m, 1] = edge[chans:]
        halo_start((m,), store, dst, send, recv)

    def stack_halo(m, above, below, into, order):
        both = jnp.concatenate([above, below], axis=0)
        for slot, step in enumerate(order):
            value = both if step == 0 else shifted(both, step)
            into[m, slot * 2 * chans : (slot + 1) * 2 * chans, :] = value

    def widened(src, m, order):
        value = src[m]
        return [value if step == 0 else shifted(value, step) for step in order]

    def convolve(taps, wide, span):
        return dot(taps[...], jnp.concatenate([value[:, span] for value in wide], axis=0))

    spans = [slice(n, n + chunk) for n in range(0, cols, chunk)]

    def get(m, span, lines=slice(None)):
        tiles = range(span.start // lane, span.stop // lane)
        return jnp.concatenate([pre[m, tile, lines, :] for tile in tiles], axis=1)

    def put(m, span, value, lines=slice(None)):
        for k, tile in enumerate(range(span.start // lane, span.stop // lane)):
            pre[m, tile, lines, :] = value[:, k * lane : (k + 1) * lane]

    for m in range(members):
        loads[m].wait()
        send_edges(m, x[m], hs, hx, hs_sem, hx_sem)
    build_forward()
    build_edges(wfh, False)
    heads.wait()

    out_k, _ = split_index((outn * rows, chans), 0, rows)
    lines = jnp.zeros((outn * rows, chans), F32)
    for k in range(outn):
        lines = jnp.where(out_k == k, out_w[k : k + 1, :].astype(F32), lines)
    lines = lines.astype(BF16)
    _, oa = split_index((outn * rows, full), 0, rows)
    _, ob = split_index((outn * rows, full), 1, rows)
    wo[...] = jnp.where(oa == ob, dot_nt(lines, spread), 0.0).astype(BF16)
    for m in range(members):
        skips[m].wait()
    for m in range(members):
        wide = widened(x, m, (-1, 0, 1))
        for span in spans:
            put(m, span, convolve(wf, wide, span) + skip[m, :, span].astype(F32))

    parts = [slice(n, n + cols // 2) for n in range(0, cols, cols // 2)]

    def gather_copy(m, part, d):
        return pltpu.make_async_remote_copy(
            src_ref=osend.at[m, :, parts[part]],
            dst_ref=ybuf.at[d, m, :, parts[part]],
            send_sem=as_sem.at[m, part, d], recv_sem=ar_sem.at[m, part, d],
            device_id={"member": lax.rem(me + d, peers)}, device_id_type=MESH,
        )

    def project(m, part):
        for n in range(parts[part].start, parts[part].stop, chunk):
            span = slice(n, n + chunk)
            value = dot(wo[...], act[m, :, span])
            outs[m, :, span] = value
            osend[m, :, span] = value.astype(BF16)
        for d in range(1, peers):
            gather_copy(m, part, d).start()

    waiting = None
    for m in range(members):
        halo_wait((m,), [(hs, hx, hs_sem, hx_sem)], "recv")
        stack_halo(m, hx[m, 0], hx[m, 1], hstk, (-1, 0, 1))
        for part, range_of in enumerate(parts):
            for n in range(range_of.start, range_of.stop, chunk):
                span = slice(n, n + chunk)
                total = get(m, span) + dot(wfh[...], hstk[m, :, span])
                put(m, span, total)
                act[m, :, span] = gelu_value(total).astype(BF16)
            if waiting is not None:
                project(*waiting)
            waiting = (m, part)
    project(*waiting)

    block = 8 * rows
    for m in range(members):
        for n in range(0, full, block):
            for span in spans:
                lines = slice(n, n + block)
                slope[m, lines, span] = gelu_slope(get(m, span, lines)).astype(BF16)
        send_edges(m, slope[m], se, hse, gs_sem, hg_sem)
    build_backward()
    build_edges(wbh, True)
    eye = (
        lax.broadcasted_iota(jnp.int32, (chans, chans), 0)
        == lax.broadcasted_iota(jnp.int32, (chans, chans), 1)
    ).astype(F32).astype(BF16)
    for k in range(outn):
        flat = jnp.broadcast_to(out_w[k : k + 1, :].astype(F32), (chunk, chans)).astype(BF16)
        wcol[k] = dot_nt(spread, flat).astype(BF16)
        wrow[k] = dot_nt(eye, flat[:lane])

    tgt.wait()
    total_members = peers * members
    for part in range(2):
        for d in range(1, peers):
            for m in range(members):
                gather_copy(m, part, d).wait_recv()
        for n in range(parts[part].start, parts[part].stop, chunk):
            span = slice(n, n + chunk)
            own = [outs[m, :, span] for m in range(members)]
            pairs = [smooth_slope(v - v) for v in own]
            for i in range(members):
                for j in range(i):
                    term = smooth_slope(own[i] - own[j])
                    pairs[i] = pairs[i] + term
                    pairs[j] = pairs[j] - term
            for d in range(1, peers):
                for j in range(members):
                    other = ybuf[d, j, :, span].astype(F32)
                    for i in range(members):
                        pairs[i] = pairs[i] + smooth_slope(own[i] - other)
            for i in range(members):
                grad = smooth_slope(own[i] - target[:, span]) - pairs[i] / (total_members - 1)
                for k in range(outn):
                    part_k = grad[k * rows : (k + 1) * rows]
                    gout[i, k, :, span] = part_k.astype(BF16)
                    gsend[i, 0, k : k + 1, span] = part_k[:1]
                    gsend[i, 1, k : k + 1, span] = part_k[rows - 1 :]

    halo_start(range(members), gsend, hgo, cs_sem, cr_sem)
    def activate(m, span):
        for n in range(0, full, rows):
            lines = slice(n, n + rows)
            grad = wcol[0, lines, :] * gout[m, 0, :, span]
            for k in range(1, outn):
                grad = grad + wcol[k, lines, :] * gout[m, k, :, span]
            act[m, lines, span] = grad * slope[m, lines, span]

    for m in range(members):
        for span in spans:
            activate(m, span)
        wide = widened(act, m, (1, 0, -1))
        for span in spans:
            put(m, span, convolve(wb, wide, span))
    halo_wait(range(members), [(se, hse, gs_sem, hg_sem), (gsend, hgo, cs_sem, cr_sem)], "recv")
    for m in range(members):
        both = []
        for half in range(2):
            tiles = []
            for c in range(0, cols, lane):
                span = slice(c, c + lane)
                grad = wrow[0] * hgo[m, half, 0:1, span].astype(BF16).astype(F32)
                for k in range(1, outn):
                    grad = grad + wrow[k] * hgo[m, half, k : k + 1, span].astype(BF16).astype(F32)
                tiles.append((grad * hse[m, half, :, span].astype(F32)).astype(BF16))
            both.append(jnp.concatenate(tiles, axis=1))
        stack_halo(m, both[0], both[1], hgk, (1, 0, -1))

    halo_wait(
        range(members),
        [(hs, hx, hs_sem, hx_sem), (se, hse, gs_sem, hg_sem), (gsend, hgo, cs_sem, cr_sem)],
        "send",
    )
    for m in range(members):
        for part in range(2):
            for d in range(1, peers):
                gather_copy(m, part, d).wait_send()


def finish(dims, pre, hgk, wbh, out_hbm, out, sem):
    members, cols, chunk = dims
    copies = []
    for m in range(members):
        for n in range(0, cols, chunk):
            span = slice(n, n + chunk)
            main = jnp.concatenate([pre[m, (n + k) // lane] for k in range(0, chunk, lane)], axis=1)
            out[m, :, span] = (main + dot(wbh[...], hgk[m, :, span])).astype(BF16)
            copy = pltpu.make_async_copy(
                out.at[m, :, span], out_hbm.at[m, :, span], sem.at[m, n // chunk]
            )
            copy.start()
            copies.append(copy)
    for copy in copies:
        copy.wait()


def local(features, skip, conv_weight, out_weight, target):
    members, chans, rows, cols = features.shape
    outn = out_weight.shape[0]
    peers = lax.axis_size("member")
    count = lax.axis_size("space")
    full = chans * rows
    chunk = min(cols, 256)
    dims = (members, chans, rows, cols, peers, count, outn, chunk)
    dma = pltpu.SemaphoreType.DMA
    anywhere = pl.BlockSpec(memory_space=pltpu.HBM)
    vmem = pl.BlockSpec(memory_space=pltpu.VMEM)
    outer = (
        pltpu.VMEM((members, cols // lane, full, lane), F32),
        pltpu.VMEM((members, 6 * chans, cols), BF16),
        pltpu.VMEM((full, 6 * chans), BF16),
    )
    held = pl.pallas_call(
        functools.partial(kernel, dims),
        out_shape=outer,
        in_specs=[anywhere] * 5,
        out_specs=(vmem, vmem, vmem),
        scratch_shapes=[
            pltpu.VMEM((members, full, cols), BF16),
            pltpu.VMEM((members, full, cols), BF16),
            pltpu.VMEM(conv_weight.shape, BF16),
            pltpu.VMEM(out_weight.shape, BF16),
            pltpu.VMEM((outn * rows, cols), F32),
            pltpu.VMEM((members, 6 * chans, cols), BF16),
            pltpu.VMEM((members, full, cols), BF16),
            pltpu.VMEM((members, full, cols), BF16),
            pltpu.VMEM((members, 2, chans, cols), BF16),
            pltpu.VMEM((members, 2, chans, cols), BF16),
            pltpu.VMEM((members, 2, chans, cols), BF16),
            pltpu.VMEM((members, 2, outn, cols), F32),
            pltpu.VMEM((members, outn * rows, cols), F32),
            pltpu.VMEM((members, outn * rows, cols), BF16),
            pltpu.VMEM((peers, members, outn * rows, cols), BF16),
            pltpu.VMEM((members, outn, rows, cols), BF16),
            pltpu.VMEM((members, 2, outn, cols), F32),
            pltpu.VMEM((members, 2, chans, cols), BF16),
            pltpu.VMEM((full, 3 * full), BF16),
            pltpu.VMEM((full, 6 * chans), BF16),
            pltpu.VMEM((full, 3 * full), BF16),
            pltpu.VMEM((3, full // lane, full, lane), F32),
            pltpu.VMEM((outn * rows, full), BF16),
            pltpu.VMEM((outn, full, chunk), BF16),
            pltpu.VMEM((outn, chans, lane), F32),
            pltpu.VMEM((2 * chans, full), BF16),
            dma((2 * members + 3,)),
            dma((members, 2)),
            dma((members, 2)),
            dma((members, 2)),
            dma((members, 2)),
            dma((members, 2, peers)),
            dma((members, 2, peers)),
            dma((members, 2)),
            dma((members, 2)),
        ],
        compiler_params=pltpu.CompilerParams(collective_id=0, has_side_effects=True, vmem_limit_bytes=58 * 2**20),
    )(
        features.reshape(members, full, cols),
        skip.reshape(members, full, cols),
        conv_weight,
        out_weight,
        target.reshape(outn * rows, cols),
    )
    result = pl.pallas_call(
        functools.partial(finish, (members, cols, chunk)),
        out_shape=jax.ShapeDtypeStruct((members, full, cols), BF16),
        in_specs=[vmem, vmem, vmem],
        out_specs=anywhere,
        scratch_shapes=[pltpu.VMEM((members, full, cols), BF16), dma((members, cols // chunk))],
        compiler_params=pltpu.CompilerParams(vmem_limit_bytes=16 * 2**20),
    )(*held)
    return result.reshape(members, chans, rows, cols)


def solution(mesh):
    placed = (
        P("member", None, "space", None),
        P("member", None, "space", None),
        P(),
        P(),
        P(None, "space", None),
    )
    return jax.shard_map(
        local,
        mesh=mesh,
        in_specs=placed,
        out_specs=P("member", None, "space", None),
        check_vma=False,
    )
```

time: 19.2 us -> 17.2 us (0.90)
  Pallas kernels: 18.1 us -> 17.1 us
  local copies, waits for them, and re-layouts: 0.97 us -> 0 us
    pallas_call x1 -> x2, Pallas kernels: 18.1 us -> 17.1 us  [the longest x1 15.8 us: local(): pl.pallas_call(functools.partial(kernel, dims), out_shape=outer, in_specs...]
    unnamed x1 -> x0, local copies, waits for them, and re-layouts: 0.97 us -> none
where the time goes in v1:
time: 17.2 us; the launch traced here: 17.1 us
  Pallas kernels  17.1 us (99%)
    pallas_call x1, Pallas kernels, local(): pl.pallas_call(functools.partial(kernel, dims), out_shape=outer, in_specs...  15.8 us
    pallas_call x1, Pallas kernels, local(): pl.pallas_call(functools.partial(finish, (members, cols, chunk)), out_sha...  1.25 us

profile of v1, /device:TPU:1, one launch (start us, length us, event | category | flops | bytes accessed | tf_op | source)
XLA Modules:
  0.0 17.1 jit_solution(13953648192302051634)
XLA Ops:
  0.0 15.8 %shard_map.55 = (f32[2,8,256,128]{3,2,1,0:T(8,128)S(1)}, bf16[2,192,1024]{2,1,0:T(8,128)(2,1)S(1)}, bf16[256,192]{1,0:T(8,128)(2,1)S(1)}) custom-call(bf16[2,256,1024]{2,1,0:T(8,128)(2,1)} %bitcast.4, bf16[2,256,1024]{2,1,0:T(8,128)(2,1)} %bitcast.5, bf16[3,3,32,32]{3,2,1,0:T(8,128)(2,1)} %weight_hbm.1, bf16[2,32]{1,0:T(2,128)(2,1)} %out_w_hbm.1, ...), custom_call_target="tpu_custom_call" | custom-call | tf_op jit(solution)/shard_map/pallas_call | solution.py:406
  15.8 1.3 %shard_map.56 = bf16[2,256,1024]{2,1,0:T(8,128)(2,1)} custom-call(f32[2,8,256,128]{3,2,1,0:T(8,128)S(1)} %get-tuple-element.8.pre, bf16[2,192,1024]{2,1,0:T(8,128)(2,1)S(1)} %get-tuple-element.9.hgk, bf16[256,192]{1,0:T(8,128)(2,1)S(1)} %get-tuple-element.10.wbh), custom_call_target="tpu_custom_call" | custom-call | tf_op jit(solution)/shard_map/pallas_call | solution.py:456

commit v2 on v1

--- a/solution.py
+++ b/solution.py
@@ -60,10 +60,10 @@
 
 
 def kernel(
-    dims, x_hbm, skip_hbm, weight_hbm, out_w_hbm, target_hbm, pre, hgk, wbh,
-    x, skip, weight, out_w, target, hstk, act, slope, hs, hx, hse, hgo, outs, osend, ybuf,
-    gout, gsend, se, wf, wfh, wb, band, wo, wcol, wrow, sel,
-    in_sem, hs_sem, hx_sem, gs_sem, hg_sem, as_sem, ar_sem, cs_sem, cr_sem,
+    dims, x_hbm, skip_hbm, weight_hbm, out_w_hbm, target_hbm, pre,
+    x, skip, weight, out_w, target, hstk, act, slope, hs, hx, hse, hgo, outs, osend, ybuf, esend, yedge,
+    gout, gsend, se, wf, wfh, wb, wbh, band, wo, woe, wcol, wrow, sel,
+    in_sem, hs_sem, hx_sem, gs_sem, hg_sem, as_sem, ar_sem, es_sem, er_sem, cs_sem, cr_sem,
 ):
     members, chans, rows, cols, peers, count, outn, chunk = dims
     full = chans * rows
@@ -105,10 +105,8 @@
         (chan == pick) & (row == jnp.where(half == 0, 0, rows - 1))
     ).astype(F32).astype(BF16)
 
-    left_chan, left_row = split_index((full, chans), 0, rows)
+    left_chan, _ = split_index((full, chans), 0, rows)
     spread = (left_chan == lax.broadcasted_iota(jnp.int32, (full, chans), 1)).astype(F32)
-    spread_first = jnp.where(left_row == 0, spread, 0.0).astype(BF16)
-    spread_last = jnp.where(left_row == rows - 1, spread, 0.0).astype(BF16)
     spread = spread.astype(BF16)
 
     def build_forward():
@@ -140,7 +138,7 @@
         slot, _ = split_index((chans, 6 * chans), 1, chans)
         first = jnp.where(slot & 1 == 0, line, 0.0).astype(BF16)
         last = jnp.where(slot & 1 == 1, line, 0.0).astype(BF16)
-        halo[...] = dot(spread_first, first).astype(BF16) + dot(spread_last, last).astype(BF16)
+        halo[...] = jnp.concatenate([first, last], axis=0)
 
     def build_backward():
         for dc in range(3):
@@ -218,6 +216,23 @@
     def convolve(taps, wide, span):
         return dot(taps[...], jnp.concatenate([value[:, span] for value in wide], axis=0))
 
+    def edge_rows(m, span):
+        tiles = range(span.start // lane, span.stop // lane)
+        halves = [
+            jnp.concatenate(
+                [pre[m, t, pl.ds(side * (rows - 1), chans, stride=rows), :] for t in tiles], axis=1
+            )
+            for side in range(2)
+        ]
+        return jnp.concatenate(halves, axis=0)
+
+    def put_edge_rows(m, span, value):
+        for side in range(2):
+            for k, t in enumerate(range(span.start // lane, span.stop // lane)):
+                pre[m, t, pl.ds(side * (rows - 1), chans, stride=rows), :] = value[
+                    side * chans : (side + 1) * chans, k * lane : (k + 1) * lane
+                ]
+
     spans = [slice(n, n + chunk) for n in range(0, cols, chunk)]
 
     def get(m, span, lines=slice(None)):
@@ -243,46 +258,82 @@
     _, oa = split_index((outn * rows, full), 0, rows)
     _, ob = split_index((outn * rows, full), 1, rows)
     wo[...] = jnp.where(oa == ob, dot_nt(lines, spread), 0.0).astype(BF16)
+    shape = (2 * outn, 2 * chans)
+    edge_k, edge_side = split_index(shape, 0, 2)
+    edge_half, _ = split_index(shape, 1, chans)
+    twice = jnp.concatenate([out_w[...].astype(F32)] * 2, axis=1)
+    lines = jnp.zeros(shape, F32)
+    for k in range(outn):
+        lines = jnp.where(edge_k == k, twice[k : k + 1], lines)
+    woe[...] = jnp.where(edge_side == edge_half, lines, 0.0).astype(BF16)
     for m in range(members):
         skips[m].wait()
-    for m in range(members):
-        wide = widened(x, m, (-1, 0, 1))
-        for span in spans:
-            put(m, span, convolve(wf, wide, span) + skip[m, :, span].astype(F32))
-
     parts = [slice(n, n + cols // 2) for n in range(0, cols, cols // 2)]
+
+    def partner(d):
+        if peers & (peers - 1):
+            return lax.rem(me + d, peers)
+        flipped, bit = 0, 1
+        while bit < peers:
+            flipped = flipped + bit * lax.rem(lax.div(me, bit) + (d // bit) % 2, 2)
+            bit *= 2
+        return flipped
+
+    def edge_copy(m, d):
+        return pltpu.make_async_remote_copy(
+            src_ref=esend.at[m], dst_ref=yedge.at[d, m],
+            send_sem=es_sem.at[m, d], recv_sem=er_sem.at[m, d],
+            device_id={"member": partner(d)}, device_id_type=MESH,
+        )
+
+    others = range(peers - 1, 0, -1)
 
     def gather_copy(m, part, d):
         return pltpu.make_async_remote_copy(
             src_ref=osend.at[m, :, parts[part]],
             dst_ref=ybuf.at[d, m, :, parts[part]],
             send_sem=as_sem.at[m, part, d], recv_sem=ar_sem.at[m, part, d],
-            device_id={"member": lax.rem(me + d, peers)}, device_id_type=MESH,
+            device_id={"member": partner(d)}, device_id_type=MESH,
         )
 
-    def project(m, part):
-        for n in range(parts[part].start, parts[part].stop, chunk):
+    def project(m, part, values):
+        for n, value in values:
             span = slice(n, n + chunk)
-            value = dot(wo[...], act[m, :, span])
+            value = dot(wo[...], value)
             outs[m, :, span] = value
             osend[m, :, span] = value.astype(BF16)
-        for d in range(1, peers):
+        for d in others:
             gather_copy(m, part, d).start()
 
     waiting = None
+    for m in range(members):
+        wide = widened(x, m, (-1, 0, 1))
+        for part, range_of in enumerate(parts):
+            values = []
+            for n in range(range_of.start, range_of.stop, chunk):
+                span = slice(n, n + chunk)
+                total = convolve(wf, wide, span) + skip[m, :, span].astype(F32)
+                put(m, span, total)
+                values.append((n, gelu_value(total).astype(BF16)))
+            if waiting is not None:
+                project(*waiting)
+            waiting = (m, part, values)
+    project(*waiting)
+
     for m in range(members):
         halo_wait((m,), [(hs, hx, hs_sem, hx_sem)], "recv")
         stack_halo(m, hx[m, 0], hx[m, 1], hstk, (-1, 0, 1))
-        for part, range_of in enumerate(parts):
-            for n in range(range_of.start, range_of.stop, chunk):
-                span = slice(n, n + chunk)
-                total = get(m, span) + dot(wfh[...], hstk[m, :, span])
-                put(m, span, total)
-                act[m, :, span] = gelu_value(total).astype(BF16)
-            if waiting is not None:
-                project(*waiting)
-            waiting = (m, part)
-    project(*waiting)
+        for span in spans:
+            total = edge_rows(m, span) + dot(wfh[...], hstk[m, :, span])
+            put_edge_rows(m, span, total)
+            value = dot(woe[...], gelu_value(total).astype(BF16))
+            esend[m, :, span] = value.astype(BF16)
+            for k in range(outn):
+                for side in range(2):
+                    row = k * rows + side * (rows - 1)
+                    outs[m, row : row + 1, span] = value[2 * k + side : 2 * k + side + 1]
+        for d in others:
+            edge_copy(m, d).start()
 
     block = 8 * rows
     for m in range(members):
@@ -304,6 +355,17 @@
 
     tgt.wait()
     total_members = peers * members
+    shape = (outn * rows, 2 * outn)
+    out_k, out_r = split_index(shape, 0, rows)
+    edge_k, edge_side = split_index(shape, 1, 2)
+    widen = (
+        (out_k == edge_k) & (out_r == jnp.where(edge_side == 0, 0, rows - 1))
+    ).astype(F32).astype(BF16)
+    _, out_r = split_index((outn * rows, chunk), 0, rows)
+    at_edge = (out_r == 0) | (out_r == rows - 1)
+    for m in range(members):
+        for d in others:
+            edge_copy(m, d).wait_recv()
     for part in range(2):
         for d in range(1, peers):
             for m in range(members):
@@ -319,7 +381,9 @@
                     pairs[j] = pairs[j] - term
             for d in range(1, peers):
                 for j in range(members):
-                    other = ybuf[d, j, :, span].astype(F32)
+                    other = jnp.where(
+                        at_edge, dot(widen, yedge[d, j, :, span]), ybuf[d, j, :, span].astype(F32)
+                    )
                     for i in range(members):
                         pairs[i] = pairs[i] + smooth_slope(own[i] - other)
             for i in range(members):
@@ -357,7 +421,9 @@
                     grad = grad + wrow[k] * hgo[m, half, k : k + 1, span].astype(BF16).astype(F32)
                 tiles.append((grad * hse[m, half, :, span].astype(F32)).astype(BF16))
             both.append(jnp.concatenate(tiles, axis=1))
-        stack_halo(m, both[0], both[1], hgk, (1, 0, -1))
+        stack_halo(m, both[0], both[1], hstk, (1, 0, -1))
+        for span in spans:
+            put_edge_rows(m, span, edge_rows(m, span) + dot(wbh[...], hstk[m, :, span]))
 
     halo_wait(
         range(members),
@@ -368,16 +434,18 @@
         for part in range(2):
             for d in range(1, peers):
                 gather_copy(m, part, d).wait_send()
-
-
-def finish(dims, pre, hgk, wbh, out_hbm, out, sem):
+        for d in others:
+            edge_copy(m, d).wait_send()
+
+
+def finish(dims, pre, out_hbm, out, sem):
     members, cols, chunk = dims
     copies = []
     for m in range(members):
         for n in range(0, cols, chunk):
             span = slice(n, n + chunk)
-            main = jnp.concatenate([pre[m, (n + k) // lane] for k in range(0, chunk, lane)], axis=1)
-            out[m, :, span] = (main + dot(wbh[...], hgk[m, :, span])).astype(BF16)
+            tiles = [pre[m, (n + k) // lane] for k in range(0, chunk, lane)]
+            out[m, :, span] = jnp.concatenate(tiles, axis=1).astype(BF16)
             copy = pltpu.make_async_copy(
                 out.at[m, :, span], out_hbm.at[m, :, span], sem.at[m, n // chunk]
             )
@@ -398,16 +466,11 @@
     dma = pltpu.SemaphoreType.DMA
     anywhere = pl.BlockSpec(memory_space=pltpu.HBM)
     vmem = pl.BlockSpec(memory_space=pltpu.VMEM)
-    outer = (
-        pltpu.VMEM((members, cols // lane, full, lane), F32),
-        pltpu.VMEM((members, 6 * chans, cols), BF16),
-        pltpu.VMEM((full, 6 * chans), BF16),
-    )
     held = pl.pallas_call(
         functools.partial(kernel, dims),
-        out_shape=outer,
+        out_shape=pltpu.VMEM((members, cols // lane, full, lane), F32),
         in_specs=[anywhere] * 5,
-        out_specs=(vmem, vmem, vmem),
+        out_specs=vmem,
         scratch_shapes=[
             pltpu.VMEM((members, full, cols), BF16),
             pltpu.VMEM((members, full, cols), BF16),
@@ -424,14 +487,18 @@
             pltpu.VMEM((members, outn * rows, cols), F32),
             pltpu.VMEM((members, outn * rows, cols), BF16),
             pltpu.VMEM((peers, members, outn * rows, cols), BF16),
+            pltpu.VMEM((members, 2 * outn, cols), BF16),
+            pltpu.VMEM((peers, members, 2 * outn, cols), BF16),
             pltpu.VMEM((members, outn, rows, cols), BF16),
             pltpu.VMEM((members, 2, outn, cols), F32),
             pltpu.VMEM((members, 2, chans, cols), BF16),
             pltpu.VMEM((full, 3 * full), BF16),
-            pltpu.VMEM((full, 6 * chans), BF16),
+            pltpu.VMEM((2 * chans, 6 * chans), BF16),
             pltpu.VMEM((full, 3 * full), BF16),
+            pltpu.VMEM((2 * chans, 6 * chans), BF16),
             pltpu.VMEM((3, full // lane, full, lane), F32),
             pltpu.VMEM((outn * rows, full), BF16),
+            pltpu.VMEM((2 * outn, 2 * chans), BF16),
             pltpu.VMEM((outn, full, chunk), BF16),
             pltpu.VMEM((outn, chans, lane), F32),
             pltpu.VMEM((2 * chans, full), BF16),
@@ -442,6 +509,8 @@
             dma((members, 2)),
             dma((members, 2, peers)),
             dma((members, 2, peers)),
+            dma((members, peers)),
+            dma((members, peers)),
             dma((members, 2)),
             dma((members, 2)),
         ],
@@ -456,11 +525,11 @@
     result = pl.pallas_call(
         functools.partial(finish, (members, cols, chunk)),
         out_shape=jax.ShapeDtypeStruct((members, full, cols), BF16),
-        in_specs=[vmem, vmem, vmem],
+        in_specs=[vmem],
         out_specs=anywhere,
         scratch_shapes=[pltpu.VMEM((members, full, cols), BF16), dma((members, cols // chunk))],
         compiler_params=pltpu.CompilerParams(vmem_limit_bytes=16 * 2**20),
-    )(*held)
+    )(held)
     return result.reshape(members, chans, rows, cols)
 
 

time: 17.2 us -> 17 us (0.988)
  Pallas kernels: 17.1 us -> 16.8 us
    pallas_call x1, Pallas kernels: 1.25 us -> 1.05 us  [local(): pl.pallas_call(functools.partial(finish, (members, cols, chunk)), out_sha...]
where the time goes in v2:
time: 17 us; the launch traced here: 16.8 us
  Pallas kernels  16.8 us (99%)
    pallas_call x1, Pallas kernels, local(): pl.pallas_call(functools.partial(kernel, dims), out_shape=pltpu.VMEM((mem...  15.8 us
    pallas_call x1, Pallas kernels, local(): pl.pallas_call(functools.partial(finish, (members, cols, chunk)), out_sha...  1.05 us

profile of v2, /device:TPU:1, one launch (start us, length us, event | category | flops | bytes accessed | tf_op | source)
XLA Modules:
  0.0 16.8 jit_solution(7279807040451301583)
XLA Ops:
  0.0 15.8 %shard_map.55.pre = f32[2,8,256,128]{3,2,1,0:T(8,128)S(1)} custom-call(bf16[2,256,1024]{2,1,0:T(8,128)(2,1)} %bitcast.4, bf16[2,256,1024]{2,1,0:T(8,128)(2,1)} %bitcast.5, bf16[3,3,32,32]{3,2,1,0:T(8,128)(2,1)} %weight_hbm.1, bf16[2,32]{1,0:T(2,128)(2,1)} %out_w_hbm.1, f32[16,1024]{1,0:T(8,128)} %bitcast.6), custom_call_target="tpu_custom_call" | custom-call | tf_op jit(solution)/shard_map/pallas_call | solution.py:469
  15.8 1.0 %shard_map.56 = bf16[2,256,1024]{2,1,0:T(8,128)(2,1)} custom-call(f32[2,8,256,128]{3,2,1,0:T(8,128)S(1)} %shard_map.55.pre), custom_call_target="tpu_custom_call" | custom-call | tf_op jit(solution)/shard_map/pallas_call | solution.py:525

commit v3 on v2

--- a/solution.py
+++ b/solution.py
@@ -61,7 +61,7 @@
 
 def kernel(
     dims, x_hbm, skip_hbm, weight_hbm, out_w_hbm, target_hbm, pre,
-    x, skip, weight, out_w, target, hstk, act, slope, hs, hx, hse, hgo, outs, osend, ybuf, esend, yedge,
+    x, skip, weight, out_w, target, hstk, act, slope, hs, hx, hse, hgo, outs, osend, ybuf, esend, yedge, oute, tedge, pedge,
     gout, gsend, se, wf, wfh, wb, wbh, band, wo, woe, wcol, wrow, sel,
     in_sem, hs_sem, hx_sem, gs_sem, hg_sem, as_sem, ar_sem, es_sem, er_sem, cs_sem, cr_sem,
 ):
@@ -75,14 +75,11 @@
     dn = {"space": lax.min(at + 1, count - 1)}
 
     loads = [pltpu.make_async_copy(x_hbm.at[m], x.at[m], in_sem.at[m]) for m in range(members)]
-    skips = [
-        pltpu.make_async_copy(skip_hbm.at[m], skip.at[m], in_sem.at[members + m])
-        for m in range(members)
-    ]
-    tgt = pltpu.make_async_copy(target_hbm, target, in_sem.at[2 * members])
-    taps = pltpu.make_async_copy(weight_hbm, weight, in_sem.at[2 * members + 1])
-    heads = pltpu.make_async_copy(out_w_hbm, out_w, in_sem.at[2 * members + 2])
-    for c in loads[:1] + [taps, heads] + loads[1:] + skips + [tgt]:
+    skips = pltpu.make_async_copy(skip_hbm, skip, in_sem.at[members])
+    tgt = pltpu.make_async_copy(target_hbm, target, in_sem.at[members + 1])
+    taps = pltpu.make_async_copy(weight_hbm, weight, in_sem.at[members + 2])
+    heads = pltpu.make_async_copy(out_w_hbm, out_w, in_sem.at[members + 3])
+    for c in loads[:1] + [taps, heads] + loads[1:] + [skips, tgt]:
         c.start()
 
     barrier = pltpu.get_barrier_semaphore()
@@ -151,41 +148,32 @@
         def _(side=side):
             for landing in (hx, hse, hgo):
                 for m in range(members):
-                    landing[m, side] = jnp.zeros(landing.shape[2:], landing.dtype)
-
-    pl.semaphore_wait(
-        barrier, peers - 1 + has_up.astype(jnp.int32) + has_dn.astype(jnp.int32)
-    )
-
-    def edge_of(src, m, half):
-        return src.at[m, half] if len(src.shape) == 4 else src.at[m]
-
-    def halo_copies(m, src, dst, send, recv):
+                    landing[side, m] = jnp.zeros(landing.shape[2:], landing.dtype)
+
+    def halo_copies(src, dst, send, recv):
         to_up = pltpu.make_async_remote_copy(
-            src_ref=edge_of(src, m, 0), dst_ref=dst.at[m, 1], send_sem=send.at[m, 0],
-            recv_sem=recv.at[m, 1], device_id=up, device_id_type=MESH,
+            src_ref=src.at[0], dst_ref=dst.at[1], send_sem=send.at[0],
+            recv_sem=recv.at[1], device_id=up, device_id_type=MESH,
         )
         to_dn = pltpu.make_async_remote_copy(
-            src_ref=edge_of(src, m, 1), dst_ref=dst.at[m, 0], send_sem=send.at[m, 1],
-            recv_sem=recv.at[m, 0], device_id=dn, device_id_type=MESH,
+            src_ref=src.at[1], dst_ref=dst.at[0], send_sem=send.at[1],
+            recv_sem=recv.at[0], device_id=dn, device_id_type=MESH,
         )
         return to_up, to_dn
 
-    def halo_start(which, src, dst, send, recv):
-        copies = [halo_copies(m, src, dst, send, recv) for m in which]
+    def halo_start(*exchange):
+        to_up, to_dn = halo_copies(*exchange)
 
         @pl.when(has_up)
         def _():
-            for to_up, _ in copies:
-                to_up.start()
+            to_up.start()
 
         @pl.when(has_dn)
         def _():
-            for _, to_dn in copies:
-                to_dn.start()
-
-    def halo_wait(which, exchanges, kind):
-        copies = [halo_copies(m, *exchange) for exchange in exchanges for m in which]
+            to_dn.start()
+
+    def halo_wait(exchanges, kind):
+        copies = [halo_copies(*exchange) for exchange in exchanges]
 
         @pl.when(has_up)
         def _():
@@ -197,11 +185,10 @@
             for to_up, to_dn in copies:
                 to_dn.wait_send() if kind == "send" else to_up.wait_recv()
 
-    def send_edges(m, source, store, dst, send, recv):
+    def extract_edges(m, source, store):
         edge = dot(sel[...], source).astype(BF16)
-        store[m, 0] = edge[:chans]
-        store[m, 1] = edge[chans:]
-        halo_start((m,), store, dst, send, recv)
+        store[0, m] = edge[:chans]
+        store[1, m] = edge[chans:]
 
     def stack_halo(m, above, below, into, order):
         both = jnp.concatenate([above, below], axis=0)
@@ -245,7 +232,11 @@
 
     for m in range(members):
         loads[m].wait()
-        send_edges(m, x[m], hs, hx, hs_sem, hx_sem)
+        extract_edges(m, x[m], hs)
+    pl.semaphore_wait(
+        barrier, peers - 1 + has_up.astype(jnp.int32) + has_dn.astype(jnp.int32)
+    )
+    halo_start(hs, hx, hs_sem, hx_sem)
     build_forward()
     build_edges(wfh, False)
     heads.wait()
@@ -259,15 +250,14 @@
     _, ob = split_index((outn * rows, full), 1, rows)
     wo[...] = jnp.where(oa == ob, dot_nt(lines, spread), 0.0).astype(BF16)
     shape = (2 * outn, 2 * chans)
-    edge_k, edge_side = split_index(shape, 0, 2)
+    edge_side, edge_k = split_index(shape, 0, outn)
     edge_half, _ = split_index(shape, 1, chans)
     twice = jnp.concatenate([out_w[...].astype(F32)] * 2, axis=1)
     lines = jnp.zeros(shape, F32)
     for k in range(outn):
         lines = jnp.where(edge_k == k, twice[k : k + 1], lines)
     woe[...] = jnp.where(edge_side == edge_half, lines, 0.0).astype(BF16)
-    for m in range(members):
-        skips[m].wait()
+    skips.wait()
     parts = [slice(n, n + cols // 2) for n in range(0, cols, cols // 2)]
 
     def partner(d):
@@ -279,20 +269,28 @@
             bit *= 2
         return flipped
 
-    def edge_copy(m, d):
+    def edge_copy(d):
         return pltpu.make_async_remote_copy(
-            src_ref=esend.at[m], dst_ref=yedge.at[d, m],
-            send_sem=es_sem.at[m, d], recv_sem=er_sem.at[m, d],
+            src_ref=esend, dst_ref=yedge.at[d],
+            send_sem=es_sem.at[d - 1], recv_sem=er_sem.at[d - 1],
             device_id={"member": partner(d)}, device_id_type=MESH,
         )
 
     others = range(peers - 1, 0, -1)
+    edges = 2 * outn
 
     def gather_copy(m, part, d):
         return pltpu.make_async_remote_copy(
             src_ref=osend.at[m, :, parts[part]],
             dst_ref=ybuf.at[d, m, :, parts[part]],
-            send_sem=as_sem.at[m, part, d], recv_sem=ar_sem.at[m, part, d],
+            send_sem=as_sem.at[d - 1], recv_sem=ar_sem.at[d - 1],
+            device_id={"member": partner(d)}, device_id_type=MESH,
+        )
+
+    def gather_whole(d):
+        return pltpu.make_async_remote_copy(
+            src_ref=osend, dst_ref=ybuf.at[d],
+            send_sem=as_sem.at[d - 1], recv_sem=ar_sem.at[d - 1],
             device_id={"member": partner(d)}, device_id_type=MESH,
         )
 
@@ -314,26 +312,25 @@
                 span = slice(n, n + chunk)
                 total = convolve(wf, wide, span) + skip[m, :, span].astype(F32)
                 put(m, span, total)
+                pedge[m, :, span] = edge_rows(m, span)
                 values.append((n, gelu_value(total).astype(BF16)))
             if waiting is not None:
                 project(*waiting)
             waiting = (m, part, values)
     project(*waiting)
 
-    for m in range(members):
-        halo_wait((m,), [(hs, hx, hs_sem, hx_sem)], "recv")
-        stack_halo(m, hx[m, 0], hx[m, 1], hstk, (-1, 0, 1))
+    halo_wait([(hs, hx, hs_sem, hx_sem)], "recv")
+    for m in range(members):
+        stack_halo(m, hx[0, m], hx[1, m], hstk, (-1, 0, 1))
+    for m in range(members):
         for span in spans:
-            total = edge_rows(m, span) + dot(wfh[...], hstk[m, :, span])
+            total = pedge[m, :, span] + dot(wfh[...], hstk[m, :, span])
             put_edge_rows(m, span, total)
             value = dot(woe[...], gelu_value(total).astype(BF16))
             esend[m, :, span] = value.astype(BF16)
-            for k in range(outn):
-                for side in range(2):
-                    row = k * rows + side * (rows - 1)
-                    outs[m, row : row + 1, span] = value[2 * k + side : 2 * k + side + 1]
-        for d in others:
-            edge_copy(m, d).start()
+            oute[m * edges : (m + 1) * edges, span] = value
+    for d in others:
+        edge_copy(d).start()
 
     block = 8 * rows
     for m in range(members):
@@ -341,7 +338,8 @@
             for span in spans:
                 lines = slice(n, n + block)
                 slope[m, lines, span] = gelu_slope(get(m, span, lines)).astype(BF16)
-        send_edges(m, slope[m], se, hse, gs_sem, hg_sem)
+        extract_edges(m, slope[m], se)
+    halo_start(se, hse, gs_sem, hg_sem)
     build_backward()
     build_edges(wbh, True)
     eye = (
@@ -355,21 +353,9 @@
 
     tgt.wait()
     total_members = peers * members
-    shape = (outn * rows, 2 * outn)
-    out_k, out_r = split_index(shape, 0, rows)
-    edge_k, edge_side = split_index(shape, 1, 2)
-    widen = (
-        (out_k == edge_k) & (out_r == jnp.where(edge_side == 0, 0, rows - 1))
-    ).astype(F32).astype(BF16)
-    _, out_r = split_index((outn * rows, chunk), 0, rows)
-    at_edge = (out_r == 0) | (out_r == rows - 1)
-    for m in range(members):
-        for d in others:
-            edge_copy(m, d).wait_recv()
+    for d in others:
+        gather_whole(d).wait_recv()
     for part in range(2):
-        for d in range(1, peers):
-            for m in range(members):
-                gather_copy(m, part, d).wait_recv()
         for n in range(parts[part].start, parts[part].stop, chunk):
             span = slice(n, n + chunk)
             own = [outs[m, :, span] for m in range(members)]
@@ -381,26 +367,53 @@
                     pairs[j] = pairs[j] - term
             for d in range(1, peers):
                 for j in range(members):
-                    other = jnp.where(
-                        at_edge, dot(widen, yedge[d, j, :, span]), ybuf[d, j, :, span].astype(F32)
-                    )
+                    other = ybuf[d, j, :, span].astype(F32)
                     for i in range(members):
                         pairs[i] = pairs[i] + smooth_slope(own[i] - other)
             for i in range(members):
                 grad = smooth_slope(own[i] - target[:, span]) - pairs[i] / (total_members - 1)
                 for k in range(outn):
                     part_k = grad[k * rows : (k + 1) * rows]
-                    gout[i, k, :, span] = part_k.astype(BF16)
-                    gsend[i, 0, k : k + 1, span] = part_k[:1]
-                    gsend[i, 1, k : k + 1, span] = part_k[rows - 1 :]
-
-    halo_start(range(members), gsend, hgo, cs_sem, cr_sem)
+                    gout[i, k, :, span] = part_k
+
+    shape = (members * edges, edges)
+    repeat = (
+        split_index(shape, 0, edges)[1] == lax.broadcasted_iota(jnp.int32, shape, 1)
+    ).astype(F32).astype(BF16)
+    for m in range(members):
+        for side in range(2):
+            for k in range(outn):
+                row = m * edges + side * outn + k
+                from_row = k * rows + side * (rows - 1)
+                tedge[row : row + 1, :] = target[from_row : from_row + 1, :]
+    for d in others:
+        edge_copy(d).wait_recv()
+    for span in spans:
+        own = oute[:, span]
+        total = jnp.zeros(own.shape, F32)
+        for j in range(members):
+            other = jnp.concatenate([own[j * edges : (j + 1) * edges]] * members, axis=0)
+            total = total + smooth_slope(own - other)
+        for d in range(1, peers):
+            for j in range(members):
+                total = total + smooth_slope(own - dot(repeat, yedge[d, j, :, span]))
+        grad = smooth_slope(own - tedge[:, span]) - total / (total_members - 1)
+        for i in range(members):
+            for side in range(2):
+                row = i * edges + side * outn
+                gsend[side, i, :, span] = grad[row : row + outn]
+                for k in range(outn):
+                    line = side * (rows - 1)
+                    gout[i, k, line : line + 1, span] = grad[row + k : row + k + 1]
+
+    halo_start(gsend, hgo, cs_sem, cr_sem)
     def activate(m, span):
+        score = [gout[m, k, :, span].astype(BF16) for k in range(outn)]
         for n in range(0, full, rows):
             lines = slice(n, n + rows)
-            grad = wcol[0, lines, :] * gout[m, 0, :, span]
+            grad = wcol[0, lines, :] * score[0]
             for k in range(1, outn):
-                grad = grad + wcol[k, lines, :] * gout[m, k, :, span]
+                grad = grad + wcol[k, lines, :] * score[k]
             act[m, lines, span] = grad * slope[m, lines, span]
 
     for m in range(members):
@@ -409,33 +422,27 @@
         wide = widened(act, m, (1, 0, -1))
         for span in spans:
             put(m, span, convolve(wb, wide, span))
-    halo_wait(range(members), [(se, hse, gs_sem, hg_sem), (gsend, hgo, cs_sem, cr_sem)], "recv")
+    halo_wait([(hs, hx, hs_sem, hx_sem), (se, hse, gs_sem, hg_sem)], "send")
+    for d in others:
+        gather_whole(d).wait_send()
+        edge_copy(d).wait_send()
+    halo_wait([(se, hse, gs_sem, hg_sem), (gsend, hgo, cs_sem, cr_sem)], "recv")
     for m in range(members):
         both = []
         for half in range(2):
             tiles = []
             for c in range(0, cols, lane):
                 span = slice(c, c + lane)
-                grad = wrow[0] * hgo[m, half, 0:1, span].astype(BF16).astype(F32)
+                grad = wrow[0] * hgo[half, m, 0:1, span].astype(BF16).astype(F32)
                 for k in range(1, outn):
-                    grad = grad + wrow[k] * hgo[m, half, k : k + 1, span].astype(BF16).astype(F32)
-                tiles.append((grad * hse[m, half, :, span].astype(F32)).astype(BF16))
+                    grad = grad + wrow[k] * hgo[half, m, k : k + 1, span].astype(BF16).astype(F32)
+                tiles.append((grad * hse[half, m, :, span].astype(F32)).astype(BF16))
             both.append(jnp.concatenate(tiles, axis=1))
         stack_halo(m, both[0], both[1], hstk, (1, 0, -1))
         for span in spans:
             put_edge_rows(m, span, edge_rows(m, span) + dot(wbh[...], hstk[m, :, span]))
 
-    halo_wait(
-        range(members),
-        [(hs, hx, hs_sem, hx_sem), (se, hse, gs_sem, hg_sem), (gsend, hgo, cs_sem, cr_sem)],
-        "send",
-    )
-    for m in range(members):
-        for part in range(2):
-            for d in range(1, peers):
-                gather_copy(m, part, d).wait_send()
-        for d in others:
-            edge_copy(m, d).wait_send()
+    halo_wait([(gsend, hgo, cs_sem, cr_sem)], "send")
 
 
 def finish(dims, pre, out_hbm, out, sem):
@@ -480,18 +487,21 @@
             pltpu.VMEM((members, 6 * chans, cols), BF16),
             pltpu.VMEM((members, full, cols), BF16),
             pltpu.VMEM((members, full, cols), BF16),
-            pltpu.VMEM((members, 2, chans, cols), BF16),
-            pltpu.VMEM((members, 2, chans, cols), BF16),
-            pltpu.VMEM((members, 2, chans, cols), BF16),
-            pltpu.VMEM((members, 2, outn, cols), F32),
+            pltpu.VMEM((2, members, chans, cols), BF16),
+            pltpu.VMEM((2, members, chans, cols), BF16),
+            pltpu.VMEM((2, members, chans, cols), BF16),
+            pltpu.VMEM((2, members, outn, cols), F32),
             pltpu.VMEM((members, outn * rows, cols), F32),
             pltpu.VMEM((members, outn * rows, cols), BF16),
             pltpu.VMEM((peers, members, outn * rows, cols), BF16),
             pltpu.VMEM((members, 2 * outn, cols), BF16),
             pltpu.VMEM((peers, members, 2 * outn, cols), BF16),
-            pltpu.VMEM((members, outn, rows, cols), BF16),
-            pltpu.VMEM((members, 2, outn, cols), F32),
-            pltpu.VMEM((members, 2, chans, cols), BF16),
+            pltpu.VMEM((members * 2 * outn, cols), F32),
+            pltpu.VMEM((members * 2 * outn, cols), F32),
+            pltpu.VMEM((members, 2 * chans, cols), F32),
+            pltpu.VMEM((members, outn, rows, cols), F32),
+            pltpu.VMEM((2, members, outn, cols), F32),
+            pltpu.VMEM((2, members, chans, cols), BF16),
             pltpu.VMEM((full, 3 * full), BF16),
             pltpu.VMEM((2 * chans, 6 * chans), BF16),
             pltpu.VMEM((full, 3 * full), BF16),
@@ -502,17 +512,17 @@
             pltpu.VMEM((outn, full, chunk), BF16),
             pltpu.VMEM((outn, chans, lane), F32),
             pltpu.VMEM((2 * chans, full), BF16),
-            dma((2 * members + 3,)),
-            dma((members, 2)),
-            dma((members, 2)),
-            dma((members, 2)),
-            dma((members, 2)),
-            dma((members, 2, peers)),
-            dma((members, 2, peers)),
-            dma((members, peers)),
-            dma((members, peers)),
-            dma((members, 2)),
-            dma((members, 2)),
+            dma((members + 4,)),
+            dma((2,)),
+            dma((2,)),
+            dma((2,)),
+            dma((2,)),
+            dma((peers - 1,)),
+            dma((peers - 1,)),
+            dma((peers - 1,)),
+            dma((peers - 1,)),
+            dma((2,)),
+            dma((2,)),
         ],
         compiler_params=pltpu.CompilerParams(collective_id=0, has_side_effects=True, vmem_limit_bytes=58 * 2**20),
     )(

time: 17 us -> 16.3 us (0.959)
  Pallas kernels: 16.8 us -> 16.1 us
    pallas_call x1, Pallas kernels: 15.8 us -> 15.1 us  [local(): pl.pallas_call(functools.partial(kernel, dims), out_shape=pltpu.VMEM((mem...]
where the time goes in v3:
time: 16.3 us; the launch traced here: 16.1 us
  Pallas kernels  16.1 us (99%)
    pallas_call x1, Pallas kernels, local(): pl.pallas_call(functools.partial(kernel, dims), out_shape=pltpu.VMEM((mem...  15.1 us
    pallas_call x1, Pallas kernels, local(): pl.pallas_call(functools.partial(finish, (members, cols, chunk)), out_sha...  1.05 us

profile of v3, /device:TPU:1, one launch (start us, length us, event | category | flops | bytes accessed | tf_op | source)
XLA Modules:
  0.0 16.1 jit_solution(8045411206832967073)
XLA Ops:
  0.0 15.1 %shard_map.55.pre = f32[2,8,256,128]{3,2,1,0:T(8,128)S(1)} custom-call(bf16[2,256,1024]{2,1,0:T(8,128)(2,1)} %bitcast.4, bf16[2,256,1024]{2,1,0:T(8,128)(2,1)} %bitcast.5, bf16[3,3,32,32]{3,2,1,0:T(8,128)(2,1)} %weight_hbm.1, bf16[2,32]{1,0:T(2,128)(2,1)} %out_w_hbm.1, f32[16,1024]{1,0:T(8,128)} %bitcast.6), custom_call_target="tpu_custom_call" | custom-call | tf_op jit(solution)/shard_map/pallas_call | solution.py:476
  15.1 1.0 %shard_map.56 = bf16[2,256,1024]{2,1,0:T(8,128)(2,1)} custom-call(f32[2,8,256,128]{3,2,1,0:T(8,128)S(1)} %shard_map.55.pre), custom_call_target="tpu_custom_call" | custom-call | tf_op jit(solution)/shard_map/pallas_call | solution.py:535

commit v4 on v3

--- a/solution.py
+++ b/solution.py
@@ -61,7 +61,7 @@
 
 def kernel(
     dims, x_hbm, skip_hbm, weight_hbm, out_w_hbm, target_hbm, pre,
-    x, skip, weight, out_w, target, hstk, act, slope, hs, hx, hse, hgo, outs, osend, ybuf, esend, yedge, oute, tedge, pedge,
+    x, skip, weight, out_w, target, act, slope, hs, hx, hse, hgo, outs, osend, ybuf, esend, yedge, oute, tedge, pedge,
     gout, gsend, se, wf, wfh, wb, wbh, band, wo, woe, wcol, wrow, sel,
     in_sem, hs_sem, hx_sem, gs_sem, hg_sem, as_sem, ar_sem, es_sem, er_sem, cs_sem, cr_sem,
 ):
@@ -190,11 +190,11 @@
         store[0, m] = edge[:chans]
         store[1, m] = edge[chans:]
 
-    def stack_halo(m, above, below, into, order):
+    def stacked(above, below, order):
         both = jnp.concatenate([above, below], axis=0)
-        for slot, step in enumerate(order):
-            value = both if step == 0 else shifted(both, step)
-            into[m, slot * 2 * chans : (slot + 1) * 2 * chans, :] = value
+        return jnp.concatenate(
+            [both if step == 0 else shifted(both, step) for step in order], axis=0
+        )
 
     def widened(src, m, order):
         value = src[m]
@@ -320,13 +320,21 @@
     project(*waiting)
 
     halo_wait([(hs, hx, hs_sem, hx_sem)], "recv")
-    for m in range(members):
-        stack_halo(m, hx[0, m], hx[1, m], hstk, (-1, 0, 1))
-    for m in range(members):
-        for span in spans:
-            total = pedge[m, :, span] + dot(wfh[...], hstk[m, :, span])
+    halos = [stacked(hx[0, m], hx[1, m], (-1, 0, 1)) for m in range(members)]
+    work = [(m, span) for m in range(members) for span in spans]
+    totals, values = {}, {}
+    for step in range(len(work) + 2):
+        if step < len(work):
+            m, span = work[step]
+            totals[step] = pedge[m, :, span] + dot(wfh[...], halos[m][:, span])
+        if 1 <= step <= len(work):
+            m, span = work[step - 1]
+            total = totals.pop(step - 1)
             put_edge_rows(m, span, total)
-            value = dot(woe[...], gelu_value(total).astype(BF16))
+            values[step - 1] = gelu_value(total).astype(BF16)
+        if step >= 2:
+            m, span = work[step - 2]
+            value = dot(woe[...], values.pop(step - 2))
             esend[m, :, span] = value.astype(BF16)
             oute[m * edges : (m + 1) * edges, span] = value
     for d in others:
@@ -427,6 +435,7 @@
         gather_whole(d).wait_send()
         edge_copy(d).wait_send()
     halo_wait([(se, hse, gs_sem, hg_sem), (gsend, hgo, cs_sem, cr_sem)], "recv")
+    halos = []
     for m in range(members):
         both = []
         for half in range(2):
@@ -438,9 +447,14 @@
                     grad = grad + wrow[k] * hgo[half, m, k : k + 1, span].astype(BF16).astype(F32)
                 tiles.append((grad * hse[half, m, :, span].astype(F32)).astype(BF16))
             both.append(jnp.concatenate(tiles, axis=1))
-        stack_halo(m, both[0], both[1], hstk, (1, 0, -1))
-        for span in spans:
-            put_edge_rows(m, span, edge_rows(m, span) + dot(wbh[...], hstk[m, :, span]))
+        halos.append(stacked(both[0], both[1], (1, 0, -1)))
+    for step in range(len(work) + 1):
+        if step < len(work):
+            m, span = work[step]
+            totals[step] = edge_rows(m, span) + dot(wbh[...], halos[m][:, span])
+        if step >= 1:
+            m, span = work[step - 1]
+            put_edge_rows(m, span, totals.pop(step - 1))
 
     halo_wait([(gsend, hgo, cs_sem, cr_sem)], "send")
 
@@ -484,7 +498,6 @@
             pltpu.VMEM(conv_weight.shape, BF16),
             pltpu.VMEM(out_weight.shape, BF16),
             pltpu.VMEM((outn * rows, cols), F32),
-            pltpu.VMEM((members, 6 * chans, cols), BF16),
             pltpu.VMEM((members, full, cols), BF16),
             pltpu.VMEM((members, full, cols), BF16),
             pltpu.VMEM((2, members, chans, cols), BF16),

time: 16.3 us -> 15.6 us (0.957)
  Pallas kernels: 16.1 us -> 15.5 us
    pallas_call x1, Pallas kernels: 15.1 us -> 14.4 us  [local(): pl.pallas_call(functools.partial(kernel, dims), out_shape=pltpu.VMEM((mem...]
where the time goes in v4:
time: 15.6 us; the launch traced here: 15.5 us
  Pallas kernels  15.5 us (99%)
    pallas_call x1, Pallas kernels, local(): pl.pallas_call(functools.partial(kernel, dims), out_shape=pltpu.VMEM((mem...  14.4 us
    pallas_call x1, Pallas kernels, local(): pl.pallas_call(functools.partial(finish, (members, cols, chunk)), out_sha...  1.05 us

profile of v4, /device:TPU:1, one launch (start us, length us, event | category | flops | bytes accessed | tf_op | source)
XLA Modules:
  0.0 15.5 jit_solution(7622226695088541198)
XLA Ops:
  0.0 14.4 %shard_map.55.pre = f32[2,8,256,128]{3,2,1,0:T(8,128)S(1)} custom-call(bf16[2,256,1024]{2,1,0:T(8,128)(2,1)} %bitcast.4, bf16[2,256,1024]{2,1,0:T(8,128)(2,1)} %bitcast.5, bf16[3,3,32,32]{3,2,1,0:T(8,128)(2,1)} %weight_hbm.1, bf16[2,32]{1,0:T(2,128)(2,1)} %out_w_hbm.1, f32[16,1024]{1,0:T(8,128)} %bitcast.6), custom_call_target="tpu_custom_call" | custom-call | tf_op jit(solution)/shard_map/pallas_call | solution.py:490
  14.4 1.0 %shard_map.56 = bf16[2,256,1024]{2,1,0:T(8,128)(2,1)} custom-call(f32[2,8,256,128]{3,2,1,0:T(8,128)S(1)} %shard_map.55.pre), custom_call_target="tpu_custom_call" | custom-call | tf_op jit(solution)/shard_map/pallas_call | solution.py:548

commit v5 on v4

--- a/solution.py
+++ b/solution.py
@@ -406,6 +406,7 @@
             for j in range(members):
                 total = total + smooth_slope(own - dot(repeat, yedge[d, j, :, span]))
         grad = smooth_slope(own - tedge[:, span]) - total / (total_members - 1)
+        grad = grad.astype(BF16).astype(F32)
         for i in range(members):
             for side in range(2):
                 row = i * edges + side * outn
@@ -430,6 +431,7 @@
         wide = widened(act, m, (1, 0, -1))
         for span in spans:
             put(m, span, convolve(wb, wide, span))
+            pedge[m, :, span] = edge_rows(m, span)
     halo_wait([(hs, hx, hs_sem, hx_sem), (se, hse, gs_sem, hg_sem)], "send")
     for d in others:
         gather_whole(d).wait_send()
@@ -442,16 +444,16 @@
             tiles = []
             for c in range(0, cols, lane):
                 span = slice(c, c + lane)
-                grad = wrow[0] * hgo[half, m, 0:1, span].astype(BF16).astype(F32)
+                grad = wrow[0] * hgo[half, m, 0:1, span]
                 for k in range(1, outn):
-                    grad = grad + wrow[k] * hgo[half, m, k : k + 1, span].astype(BF16).astype(F32)
+                    grad = grad + wrow[k] * hgo[half, m, k : k + 1, span]
                 tiles.append((grad * hse[half, m, :, span].astype(F32)).astype(BF16))
             both.append(jnp.concatenate(tiles, axis=1))
         halos.append(stacked(both[0], both[1], (1, 0, -1)))
     for step in range(len(work) + 1):
         if step < len(work):
             m, span = work[step]
-            totals[step] = edge_rows(m, span) + dot(wbh[...], halos[m][:, span])
+            totals[step] = pedge[m, :, span] + dot(wbh[...], halos[m][:, span])
         if step >= 1:
             m, span = work[step - 1]
             put_edge_rows(m, span, totals.pop(step - 1))

time: 15.6 us -> 15.6 us (level)
  no operation moved by 1% of the time
where the time goes in v5:
time: 15.6 us; the launch traced here: 15.5 us
  Pallas kernels  15.5 us (99%)
    pallas_call x1, Pallas kernels, local(): pl.pallas_call(functools.partial(kernel, dims), out_shape=pltpu.VMEM((mem...  14.4 us
    pallas_call x1, Pallas kernels, local(): pl.pallas_call(functools.partial(finish, (members, cols, chunk)), out_sha...  1.05 us

profile of v5, /device:TPU:1, one launch (start us, length us, event | category | flops | bytes accessed | tf_op | source)
XLA Modules:
  0.0 15.5 jit_solution(10298091631115625841)
XLA Ops:
  0.0 14.4 %shard_map.55.pre = f32[2,8,256,128]{3,2,1,0:T(8,128)S(1)} custom-call(bf16[2,256,1024]{2,1,0:T(8,128)(2,1)} %bitcast.4, bf16[2,256,1024]{2,1,0:T(8,128)(2,1)} %bitcast.5, bf16[3,3,32,32]{3,2,1,0:T(8,128)(2,1)} %weight_hbm.1, bf16[2,32]{1,0:T(2,128)(2,1)} %out_w_hbm.1, f32[16,1024]{1,0:T(8,128)} %bitcast.6), custom_call_target="tpu_custom_call" | custom-call | tf_op jit(solution)/shard_map/pallas_call | solution.py:492
  14.4 1.0 %shard_map.56 = bf16[2,256,1024]{2,1,0:T(8,128)(2,1)} custom-call(f32[2,8,256,128]{3,2,1,0:T(8,128)S(1)} %shard_map.55.pre), custom_call_target="tpu_custom_call" | custom-call | tf_op jit(solution)/shard_map/pallas_call | solution.py:550
